TPU v7x, 256 devices: a whole 4x4x8 slice. The times are simulated.
256 devices in a mesh: wide: 64 (over z, x, core), narrow: 4 (over y).
Axes of the slice: x: 4, y: 4, z: 8, core: 2. Of those that a mesh axis runs over, the one named last changes fastest.
Arguments:
- snapshot: float32 [512, 16, 512, 128], P('wide', 'narrow'), may hold values from -81 to 81
Outputs:
- core: float32 [256, 16, 512, 128], P(None, 'narrow', 'wide')
- factor: float32 [512, 256], replicated
All inputs are finite; a program needn't handle non-finite values.
Results may differ from a plain program's by a relative error of at most 0.000071.
Values sent between devices are 32-bit elements; how exact they have to be, the bound alone decides.
A program may use at most 320 MiB of HBM per device.

v0:
```python
import jax
import jax.numpy as jnp
from jax import lax
from jax.sharding import PartitionSpec as P

RANK = 256


def on_device(snapshot):
    regrouped = lax.all_to_all(snapshot, "wide", split_axis=2, concat_axis=0, tiled=True)
    rows_all = regrouped.shape[0]
    unfold = regrouped.reshape(rows_all, -1)
    gram = jnp.dot(
        unfold, unfold.T, precision=lax.Precision.HIGHEST, preferred_element_type=jnp.float32
    )
    gram = lax.psum(gram, "narrow")
    gram = lax.psum(gram, "wide")
    upper = jnp.linalg.cholesky(gram).T
    rows_kept = upper[:RANK, :]
    lengths = jnp.sqrt(jnp.sum(rows_kept * rows_kept, axis=1))
    factor = (rows_kept / lengths[:, None]).T
    core = jnp.dot(
        factor.T, unfold, precision=lax.Precision.HIGHEST, preferred_element_type=jnp.float32
    )
    core = core.reshape(RANK, regrouped.shape[1], regrouped.shape[2], regrouped.shape[3])
    return (core, factor)


def solution(mesh):
    in_specs = (P("wide", "narrow", None, None),)
    out_specs = (P(None, "narrow", "wide", None), P())
    return jax.shard_map(
        on_device, mesh=mesh, in_specs=in_specs, out_specs=out_specs, check_vma=False
    )
```

profile of v0, /device:TPU:2, one launch (start us, length us, event | category | flops | bytes accessed | tf_op | source)
XLA Modules:
  0.0 603.6 jit_solution(17001077467662318990)
XLA Ops:
  7.2 0.0 all-reduce.4.cloned.1.call-start
  7.2 8.2 %copy.21 = f32[8,4,512,128]{3,0,1,2:T(8,128)S(1)} copy(f32[8,4,512,128]{3,2,1,0:T(8,128)} %param.1) | data formatting | bytes 16777216 | tf_op args[0]
  15.4 198.1 %all_to_all.15 = f32[8,4,512,128]{3,0,1,2:T(8,128)S(1)} all-to-all(f32[8,4,512,128]{3,0,1,2:T(8,128)S(1)} %copy.21), channel_id=1, replica_groups=mesh['wide'=64,'narrow'=4] {'wide'}, dimensions={2} | all-to-all | bytes 16777216 | tf_op jit(solution)/shard_map/all_to_all | solution.py:10
  213.5 11.3 %copy.32 = f32[8,4,64,8,128]{4,3,1,0,2:T(8,128)} copy(f32[8,4,64,8,128]{4,0,1,3,2:T(8,128)S(1)} %bitcast.42) | data formatting | bytes 16777216 | tf_op jit(solution)/shard_map/all_to_all | solution.py:10
  224.8 9.4 %reshape.40 = f32[512,4096]{1,0:T(8,128)} reshape(f32[64,8,4,8,128]{4,3,2,1,0:T(8,128)} %bitcast.43) | data formatting | bytes 16777216 | tf_op jit(solution)/shard_map/reshape | solution.py:12
  234.2 17.2 %fusion.15 = f32[512,512]{0,1:T(8,128)} fusion(f32[512,4096]{1,0:T(8,128)} %reshape.40), kind=kOutput, calls=%fused_computation.43 | convolution fusion | flops 12884901888 | bytes 9437184 | tf_op jit(solution)/shard_map/dot_general | solution.py:13
  251.5 0.0 all-reduce.4.cloned.1.call-update
  251.5 0.0 all-reduce.6.cloned.1.call-start
  251.5 47.4 %all-reduce.4.cloned.1.call-done = f32[512,512]{0,1:T(8,128)} async-done(((f32[512,512]{0,1:T(8,128)}), f32[512,512]{0,1:T(8,128)}) %all-reduce.4.cloned.1.call-update) | async-done | bytes 1048592 | tf_op jit(solution)/shard_map/psum | solution.py:16
  299.0 0.0 all-reduce.6.cloned.1.call-update
  299.0 9.4 %copy.25 = f32[4096,512]{1,0:T(8,128)} copy(f32[4096,512]{0,1:T(8,128)} %bitcast.40) | data formatting | bytes 16777216 | tf_op jit(solution)/shard_map/dot_general | solution.py:22
  308.4 180.5 %all-reduce.6.cloned.1.call-done = f32[512,512]{0,1:T(8,128)} async-done(((f32[512,512]{0,1:T(8,128)}), f32[512,512]{0,1:T(8,128)}) %all-reduce.6.cloned.1.call-update) | async-done | bytes 1048592 | tf_op jit(solution)/shard_map/psum | solution.py:17
  488.9 1.6 copy.24
  490.4 1.4 fusion
  491.9 11.7 %cholesky.104 = f32[128,128]{1,0:T(8,128)S(1)} custom-call(f32[128,128]{1,0:T(8,128)S(1)} %cholesky.266), custom_call_target="Cholesky" | custom-call | tf_op jit(solution)/shard_map/jit(cholesky)/cholesky | solution.py:18
  503.7 0.1 cholesky.224
  503.8 9.8 %custom-call.27 = f32[1,128,128]{1,2,0:T(8,128)S(1)} custom-call(f32[1,128,128]{2,1,0:T(8,128)S(1)} %get-tuple-element.19), custom_call_target="InvertDiagBlocksLowerTriangular" | custom-call | tf_op jit(solution)/shard_map/jit(cholesky)/cholesky | solution.py:18
  513.6 0.3 constant_dynamic-update-slice_fusion.2
  513.9 0.3 convolution_subtract_fusion
  514.3 11.7 %cholesky.217 = f32[128,128]{1,0:T(8,128)S(1)} custom-call(f32[128,128]{1,0:T(8,128)S(1)} %cholesky.270), custom_call_target="Cholesky" | custom-call | tf_op jit(solution)/shard_map/jit(cholesky)/cholesky | solution.py:18
  526.0 10.0 %custom-call.28 = f32[1,128,128]{1,2,0:T(8,128)S(1)} custom-call(f32[1,128,128]{2,1,0:T(8,128)S(1)} %get-tuple-element.16), custom_call_target="InvertDiagBlocksLowerTriangular" | custom-call | tf_op jit(solution)/shard_map/jit(cholesky)/cholesky | solution.py:18
  536.0 0.3 convolution_dynamic-update-slice_fusion
  536.3 0.4 convolution_subtract_fusion.1
  536.7 11.7 %cholesky.238 = f32[128,128]{1,0:T(8,128)S(1)} custom-call(f32[128,128]{1,0:T(8,128)S(1)} %cholesky.275), custom_call_target="Cholesky" | custom-call | tf_op jit(solution)/shard_map/jit(cholesky)/cholesky | solution.py:18
  548.4 9.8 %custom-call.29 = f32[1,128,128]{1,2,0:T(8,128)S(1)} custom-call(f32[1,128,128]{2,1,0:T(8,128)S(1)} %get-tuple-element.13), custom_call_target="InvertDiagBlocksLowerTriangular" | custom-call | tf_op jit(solution)/shard_map/jit(cholesky)/cholesky | solution.py:18
  558.2 0.2 convolution_dynamic-update-slice_fusion.1
  558.4 0.4 convolution_subtract_fusion.2
  558.8 11.7 %cholesky.255 = f32[128,128]{1,0:T(8,128)S(1)} custom-call(f32[128,128]{1,0:T(8,128)S(1)} %convolution_subtract_fusion.2), custom_call_target="Cholesky" | custom-call | tf_op jit(solution)/shard_map/jit(cholesky)/cholesky | solution.py:18
  570.6 0.6 compare_reduce_fusion.1
  571.2 0.6 compare_reduce_fusion
  571.8 0.6 compare_reduce_fusion.2
  575.0 0.1 select_bitcast_fusion
  575.1 0.3 multiply_reduce_fusion
  575.4 0.9 fusion.7
  576.3 15.8 %fusion.1 = f32[256,4,8,128]{3,0,2,1:T(8,128)S(1)} fusion(f32[4,8,128,512]{3,2,1,0:T(8,128)} %bitcast.41, f32[512,512]{0,1:T(8,128)S(1)} %select_bitcast_fusion, f32[256]{0:T(256)S(1)} %sqrt.7), kind=kOutput, calls=%fused_computation.10 | convolution fusion | flops 6442582016 | bytes 13108224 | tf_op jit(solution)/shard_map/dot_general | solution.py:22
  592.1 4.4 copy.27
  (8 shorter events, 0.2 us)
Async XLA Ops:
  7.2 291.8 %all-reduce.4.cloned.1.call-start = ((), (), s32[]{:S(2)}) async-start(), calls=%async_computation.1 | async-start | bytes 2097152 | tf_op jit(solution)/shard_map/psum | solution.py:16
  251.5 237.4 %all-reduce.6.cloned.1.call-start = ((), (), s32[]{:S(2)}) async-start(), calls=%async_computation.2 | async-start | bytes 2097152 | tf_op jit(solution)/shard_map/psum | solution.py:17
Sparse Core Ops, SparseCore 0:
  251.6 47.3 all-reduce.3
  302.8 186.0 all-reduce.5
where the time goes:
time: 609 us; the launch traced here: 604 us
  waiting for transfers between devices  228 us (37%)
  blocking collectives  198 us (33%)
  other arithmetic  81.2 us (13%)
  local copies, waits for them, and re-layouts  44.5 us (7%)
  matrix products  34.9 us (6%)
  between operations  16.9 us (3%)
    all_to_all x1, blocking collectives, on_device(): lax.all_to_all(snapshot, 'wide', split_axis=2, concat_axis=0, tiled=True)  198 us
    psum x1, waiting for transfers between devices, on_device(): gram = lax.psum(gram, 'wide')  180 us
    another operation x14, other arithmetic, on_device(): upper = jnp.linalg.cholesky(gram).T  78.5 us
    psum x1, waiting for transfers between devices, on_device(): gram = lax.psum(gram, 'narrow')  47.4 us
    dot_general x1, matrix products, on_device(): jnp.dot(unfold, unfold.T, precision=lax.Precision.HIGHEST, preferred_elem...  17.2 us
    dot_general x1, matrix products, on_device(): jnp.dot(factor.T, unfold, precision=lax.Precision.HIGHEST, preferred_elem...  15.8 us
    unnamed x2, local copies, waits for them, and re-layouts  12.7 us
  transfers between devices with their start and end apart: 2, of which 2 were waited for; matrix products, arithmetic and copies ran while one was open for 2% of the time, Pallas kernels for 0%

commit v1 on v0

--- a/solution.py
+++ b/solution.py
@@ -1,9 +1,18 @@
+import functools
 import jax
 import jax.numpy as jnp
 from jax import lax
 from jax.sharding import PartitionSpec as P
+from jax.lax import all_gather
 
 RANK = 256
+
+
+def recast_patches(patch, chip_axis):
+    return jnp.sum(all_gather(patch, chip_axis), 0)
+
+
+handle_targets = functools.partial(recast_patches, chip_axis="wide")
 
 
 def on_device(snapshot):
@@ -14,7 +23,7 @@
         unfold, unfold.T, precision=lax.Precision.HIGHEST, preferred_element_type=jnp.float32
     )
     gram = lax.psum(gram, "narrow")
-    gram = lax.psum(gram, "wide")
+    gram = handle_targets(gram)
     upper = jnp.linalg.cholesky(gram).T
     rows_kept = upper[:RANK, :]
     lengths = jnp.sqrt(jnp.sum(rows_kept * rows_kept, axis=1))

time: 609 us -> 680 us (1.12)
  waiting for transfers between devices: 228 us -> 277 us
  other arithmetic: 81.2 us -> 101 us
    all_gather x0 -> x1, waiting for transfers between devices: none -> 230 us  [recast_patches(): return jnp.sum(all_gather(patch, chip_axis), 0)]
    psum x1 -> x0, waiting for transfers between devices: 180 us -> none  [on_device(): gram = lax.psum(gram, 'wide')]
    reduce_sum x0 -> x1, other arithmetic: none -> 21.2 us  [recast_patches(): return jnp.sum(all_gather(patch, chip_axis), 0)]
  transfers between devices with their start and end apart: 2 -> 2, of which waited for: 2 -> 2; matrix products, arithmetic and copies ran while one was open for 2% -> 1% of each run, Pallas kernels for 0% -> 0%
where the time goes in v1:
time: 680 us; the launch traced here: 672 us
  waiting for transfers between devices  277 us (41%)
  blocking collectives  198 us (29%)
  other arithmetic  101 us (15%)
  local copies, waits for them, and re-layouts  42.9 us (6%)
  matrix products  35 us (5%)
  between operations  17 us (2%)
    all_gather x1, waiting for transfers between devices, recast_patches(): return jnp.sum(all_gather(patch, chip_axis), 0)  230 us
    all_to_all x1, blocking collectives, on_device(): lax.all_to_all(snapshot, 'wide', split_axis=2, concat_axis=0, tiled=True)  198 us
    another operation x14, other arithmetic, on_device(): upper = jnp.linalg.cholesky(gram).T  78.5 us
    psum x1, waiting for transfers between devices, on_device(): gram = lax.psum(gram, 'narrow')  47.4 us
    reduce_sum x1, other arithmetic, recast_patches(): return jnp.sum(all_gather(patch, chip_axis), 0)  21.2 us
    dot_general x1, matrix products, on_device(): jnp.dot(unfold, unfold.T, precision=lax.Precision.HIGHEST, preferred_elem...  17.3 us
    dot_general x1, matrix products, on_device(): jnp.dot(factor.T, unfold, precision=lax.Precision.HIGHEST, preferred_elem...  15.8 us
  transfers between devices with their start and end apart: 2, of which 2 were waited for; matrix products, arithmetic and copies ran while one was open for 1% of the time, Pallas kernels for 0%

profile of v1, /device:TPU:2, one launch (start us, length us, event | category | flops | bytes accessed | tf_op | source)
XLA Modules:
  0.0 671.8 jit_solution(659521183995401789)
XLA Ops:
  7.2 0.0 all-reduce.3.cloned.1.call-start
  7.2 8.2 %copy.18 = f32[8,4,512,128]{3,0,1,2:T(8,128)S(1)} copy(f32[8,4,512,128]{3,2,1,0:T(8,128)} %param.1) | data formatting | bytes 16777216 | tf_op args[0]
  15.4 198.1 %all_to_all.15 = f32[8,4,512,128]{3,0,1,2:T(8,128)S(1)} all-to-all(f32[8,4,512,128]{3,0,1,2:T(8,128)S(1)} %copy.18), channel_id=1, replica_groups=mesh['wide'=64,'narrow'=4] {'wide'}, dimensions={2} | all-to-all | bytes 16777216 | tf_op jit(solution)/shard_map/all_to_all | solution.py:19
  213.5 11.3 %copy.27 = f32[8,4,64,8,128]{4,3,1,0,2:T(8,128)} copy(f32[8,4,64,8,128]{4,0,1,3,2:T(8,128)S(1)} %bitcast.44) | data formatting | bytes 16777216 | tf_op jit(solution)/shard_map/all_to_all | solution.py:19
  224.8 9.4 %reshape.40 = f32[512,4096]{1,0:T(8,128)} reshape(f32[64,8,4,8,128]{4,3,2,1,0:T(8,128)} %bitcast.45) | data formatting | bytes 16777216 | tf_op jit(solution)/shard_map/reshape | solution.py:21
  234.2 17.3 %convolution_bitcast_fusion = f32[1,512,512]{2,1,0:T(8,128)} fusion(f32[512,4096]{1,0:T(8,128)} %reshape.40), kind=kOutput, calls=%fused_computation.1 | convolution fusion | flops 12884901888 | bytes 9437184 | tf_op jit(solution)/shard_map/dot_general | solution.py:22
  251.6 0.0 all-reduce.3.cloned.1.call-update
  251.6 0.0 all-gather.2.cloned.1.call-start
  251.6 47.4 %all-reduce.3.cloned.1.call-done = f32[1,512,512]{2,1,0:T(8,128)} async-done(((f32[1,512,512]{2,1,0:T(8,128)}), f32[1,512,512]{2,1,0:T(8,128)}) %all-reduce.3.cloned.1.call-update) | async-done | bytes 1048592 | tf_op jit(solution)/shard_map/psum | solution.py:25
  299.1 0.0 all-gather.2.cloned.1.call-update
  299.1 9.0 %copy.21 = f32[4096,512]{1,0:T(8,128)} copy(f32[4096,512]{0,1:T(8,128)} %bitcast.42) | data formatting | bytes 16777216 | tf_op jit(solution)/shard_map/dot_general | solution.py:31
  308.1 230.0 %all-gather.2.cloned.1.call-done = f32[64,512,512]{2,1,0:T(8,128)} async-done(((f32[1,512,512]{2,1,0:T(8,128)}), f32[64,512,512]{2,1,0:T(8,128)}) %all-gather.2.cloned.1.call-update) | async-done | bytes 67108880 | tf_op jit(solution)/shard_map/all_gather | solution.py:12
  538.2 21.2 %reduce_sum.18 = f32[512,512]{1,0:T(8,128)S(1)} reduce(f32[64,512,512]{2,1,0:T(8,128)} %all-gather.2.cloned.1.call-done, f32[]{:T(128)} %constant.130.clone.1), dimensions={0}, to_apply=%region_1.0 | reduce | flops 16515072 | bytes 68157440 | tf_op jit(solution)/shard_map/reduce_sum | solution.py:12
  559.4 0.3 copy.20
  559.7 0.2 fusion
  560.0 11.7 %cholesky.104 = f32[128,128]{1,0:T(8,128)S(1)} custom-call(f32[128,128]{1,0:T(8,128)S(1)} %cholesky.266), custom_call_target="Cholesky" | custom-call | tf_op jit(solution)/shard_map/jit(cholesky)/cholesky | solution.py:27
  571.7 0.1 cholesky.224
  571.9 9.8 %custom-call.27 = f32[1,128,128]{1,2,0:T(8,128)S(1)} custom-call(f32[1,128,128]{2,1,0:T(8,128)S(1)} %get-tuple-element.19), custom_call_target="InvertDiagBlocksLowerTriangular" | custom-call | tf_op jit(solution)/shard_map/jit(cholesky)/cholesky | solution.py:27
  581.7 0.3 constant_dynamic-update-slice_fusion.2
  582.0 0.3 convolution_subtract_fusion
  582.4 11.7 %cholesky.217 = f32[128,128]{1,0:T(8,128)S(1)} custom-call(f32[128,128]{1,0:T(8,128)S(1)} %cholesky.270), custom_call_target="Cholesky" | custom-call | tf_op jit(solution)/shard_map/jit(cholesky)/cholesky | solution.py:27
  594.1 9.9 %custom-call.28 = f32[1,128,128]{1,2,0:T(8,128)S(1)} custom-call(f32[1,128,128]{2,1,0:T(8,128)S(1)} %get-tuple-element.16), custom_call_target="InvertDiagBlocksLowerTriangular" | custom-call | tf_op jit(solution)/shard_map/jit(cholesky)/cholesky | solution.py:27
  604.0 0.3 convolution_dynamic-update-slice_fusion
  604.3 0.4 convolution_subtract_fusion.1
  604.7 11.7 %cholesky.238 = f32[128,128]{1,0:T(8,128)S(1)} custom-call(f32[128,128]{1,0:T(8,128)S(1)} %cholesky.275), custom_call_target="Cholesky" | custom-call | tf_op jit(solution)/shard_map/jit(cholesky)/cholesky | solution.py:27
  616.5 0.7 compare_reduce_fusion.1
  617.2 9.8 %custom-call.29 = f32[1,128,128]{1,2,0:T(8,128)S(1)} custom-call(f32[1,128,128]{2,1,0:T(8,128)S(1)} %get-tuple-element.13), custom_call_target="InvertDiagBlocksLowerTriangular" | custom-call | tf_op jit(solution)/shard_map/jit(cholesky)/cholesky | solution.py:27
  627.0 0.2 convolution_dynamic-update-slice_fusion.1
  627.2 0.4 convolution_subtract_fusion.2
  627.6 11.7 %cholesky.255 = f32[128,128]{1,0:T(8,128)S(1)} custom-call(f32[128,128]{1,0:T(8,128)S(1)} %convolution_subtract_fusion.2), custom_call_target="Cholesky" | custom-call | tf_op jit(solution)/shard_map/jit(cholesky)/cholesky | solution.py:27
  639.3 0.6 compare_reduce_fusion
  640.0 0.6 compare_reduce_fusion.2
  643.2 0.1 select_bitcast_fusion
  643.3 0.3 multiply_reduce_fusion
  643.6 0.9 fusion.7
  644.5 15.8 %fusion.1 = f32[256,4,8,128]{3,0,2,1:T(8,128)S(1)} fusion(f32[4,8,128,512]{3,2,1,0:T(8,128)} %bitcast.43, f32[512,512]{0,1:T(8,128)S(1)} %select_bitcast_fusion, f32[256]{0:T(256)S(1)} %sqrt.7), kind=kOutput, calls=%fused_computation.11 | convolution fusion | flops 6442582016 | bytes 13108224 | tf_op jit(solution)/shard_map/dot_general | solution.py:31
  660.3 4.4 copy.23
  (8 shorter events, 0.2 us)
Async XLA Ops:
  7.2 291.9 %all-reduce.3.cloned.1.call-start = ((), (), s32[]{:S(2)}) async-start(), calls=%async_computation.1 | async-start | bytes 2097152 | tf_op jit(solution)/shard_map/psum | solution.py:25
  251.6 286.6 %all-gather.2.cloned.1.call-start = ((), (), s32[]{:S(2)}) async-start(), calls=%async_computation.2 | async-start | bytes 68157440 | tf_op jit(solution)/shard_map/all_gather | solution.py:12
Sparse Core Ops, SparseCore 0:
  251.7 47.3 all-reduce.2
  302.2 235.8 all-gather.1
